TPU v7x, 32 devices: a whole 2x2x4 slice. The times are simulated.
32 devices in a mesh: tm: 8 (over z, core), dp: 2 (over y), rep: 2 (over x).
Axes of the slice: x: 2, y: 2, z: 4, core: 2. Of those that a mesh axis runs over, the one named last changes fastest.
Arguments:
- clip_frames: bfloat16 [4, 32, 8, 4, 256], P(('dp', 'rep'), 'tm'), may hold values from -6 to 6
- conv_weight: bfloat16 [3, 3, 3, 256, 256], replicated, may hold values from -0.078125 to 0.078125
- up_weight: bfloat16 [256, 1024], replicated, may hold values from -0.375 to 0.375
- cotangent: bfloat16 [4, 32, 8, 4, 1024], P(('dp', 'rep'), None, 'tm'), may hold values from -6 to 6
Outputs:
- input_grad: bfloat16 [4, 32, 8, 4, 256], P(('dp', 'rep'), 'tm')
- up_grad: float32 [256, 1024], P('tm', ('dp', 'rep'))
All inputs are finite; a program needn't handle non-finite values.
Results may differ from a plain program's by a relative error of at most 0.012.
Values may be sent and summed in bfloat16 or wider, within the bound.
No kernel may reach another device: no remote copies, remote signals or barrier semaphores. Data moves between devices by JAX's collectives and lax.ppermute only.
A program may use at most 128 MiB of HBM per device.

v0:
```python
import math
import jax
import jax.numpy as jnp
from jax import lax
from jax.sharding import PartitionSpec as P


def from_behind(value, axis, steps):
    count = lax.axis_size(axis)
    initial, last = (max(0, -steps), min(count, count - steps))
    return lax.ppermute(value, axis, [(source, source + steps) for source in range(initial, last)])


def correlate(source, kernel, frames):
    rows = source.shape[1] - 2
    cols = source.shape[2] - 2
    patches = []
    for shift_t in range(3):
        for shift_r in range(3):
            for shift_c in range(3):
                patches.append(
                    source[
                        shift_t : shift_t + frames,
                        shift_r : shift_r + rows,
                        shift_c : shift_c + cols,
                    ]
                )
    stacked = jnp.concatenate(patches, axis=-1)
    width = stacked.shape[-1]
    flat_kernel = kernel.reshape(width, kernel.shape[-1])
    return jnp.dot(stacked.reshape(-1, width), flat_kernel, preferred_element_type=jnp.float32)


def pad_space(field):
    return jnp.pad(field, ((0, 0), (1, 1), (1, 1), (0, 0)))


def local(clip_frames, conv_weight, up_weight, cotangent):
    frames_local = clip_frames[0]
    frames = frames_local.shape[0]
    rows = frames_local.shape[1]
    cols = frames_local.shape[2]
    chans = frames_local.shape[3]
    is_first = lax.axis_index("tm") == 0
    earlier = from_behind(frames_local[frames - 2 :], "tm", 1)
    earlier = jnp.where(is_first, jnp.broadcast_to(frames_local[:1], earlier.shape), earlier)
    source = pad_space(jnp.concatenate([earlier, frames_local], axis=0))
    pre = correlate(source, conv_weight, frames)
    hidden = jax.nn.silu(pre).astype(jnp.bfloat16).reshape(1, frames, rows, cols, chans)
    contract_rows = (((0,), (0,)), ((), ()))
    contract_cols = (((1,), (1,)), ((), ()))
    frame_cot = lax.all_to_all(cotangent, "tm", split_axis=1, concat_axis=2, tiled=True)
    flat_g = frame_cot.reshape(-1, frame_cot.shape[-1])
    term = lax.dot_general(
        hidden.reshape(-1, chans), flat_g, contract_rows, preferred_element_type=jnp.float32
    )
    hidden_grad = lax.dot_general(
        flat_g, up_weight, contract_cols, preferred_element_type=jnp.float32
    ).astype(jnp.bfloat16)
    sigma = jax.nn.sigmoid(pre)
    slope = sigma * (1.0 + pre * (1.0 - sigma))
    pre_grad = (hidden_grad.astype(jnp.float32) * slope).astype(jnp.bfloat16)
    pre_grad = pre_grad.reshape(frames, rows, cols, chans)
    later = from_behind(pre_grad[:2], "tm", -1)
    back_kernel = jnp.transpose(conv_weight[::-1, ::-1, ::-1], (0, 1, 2, 4, 3))
    grad_source = pad_space(jnp.concatenate([pre_grad, later], axis=0))
    input_grad = correlate(grad_source, back_kernel, frames).reshape(frames, rows, cols, chans)

    def edge_term():
        start = jnp.concatenate(
            [jnp.zeros((2, rows, cols, chans), jnp.bfloat16), pre_grad[:2]], axis=0
        )
        parts = correlate(pad_space(start), back_kernel, 2).reshape(2, rows, cols, chans)
        return parts[0] + parts[1]

    def no_term():
        return jnp.zeros((rows, cols, chans), jnp.float32)

    edge = lax.cond(is_first, edge_term, no_term)
    input_grad = input_grad.at[0].add(edge)
    time_count = lax.axis_size("tm")
    clip_count = lax.axis_size(("dp", "rep"))
    factor = 1.0 / math.sqrt(clip_count * frames * time_count * rows * cols)
    part = lax.psum_scatter(term, "tm", scatter_dimension=0, tiled=True)
    summed = lax.psum_scatter(part, ("dp", "rep"), scatter_dimension=1, tiled=True)
    return (input_grad.astype(jnp.bfloat16)[None], summed * factor)


def solution(mesh):
    in_specs = (
        P(("dp", "rep"), "tm", None, None, None),
        P(),
        P(),
        P(("dp", "rep"), None, "tm", None, None),
    )
    out_specs = (P(("dp", "rep"), "tm", None, None, None), P("tm", ("dp", "rep")))
    return jax.shard_map(local, mesh=mesh, in_specs=in_specs, out_specs=out_specs, check_vma=False)
```

profile of v0, /device:TPU:0, one launch (start us, length us, event | category | flops | bytes accessed | tf_op | source)
XLA Modules:
  0.0 133.0 jit_solution(5692337568943609760)
XLA Ops:
  7.2 0.0 copy-start
  7.2 0.8 slice_bitcast_fusion
  8.0 2.4 %collective-permute-start = (bf16[2,8,4,256]{3,2,1,0:T(4,128)(2,1)S(1)}, bf16[2,8,4,256]{3,2,1,0:T(4,128)(2,1)S(1)}, u32[]{:S(2)}, u32[]{:S(2)}) collective-permute-start(bf16[2,8,4,256]{3,2,1,0:T(4,128)(2,1)S(1)} %slice_bitcast_fusion), channel_id=1, source_target_pairs={{0,4},{4,8},{8,12},{12,16},{16,20},{20,24},{24,28},{1,5},{5,9},{9,... | collective-permute-start | bytes 98312 | tf_op jit(solution)/shard_map/ppermute | solution.py:11
  10.4 6.2 %all-to-all-start = ((bf16[1,32,1,4,1024]{4,3,2,0,1:T(4,128)(2,1)}), bf16[1,32,1,4,1024]{4,3,2,0,1:T(4,128)(2,1)S(1)}, u32[]{:S(2)}, u32[]{:S(2)}) async-start(bf16[1,32,1,4,1024]{4,3,2,0,1:T(4,128)(2,1)} %bitcast.45), calls=%async_computation | async-start | bytes 524288 | tf_op jit(solution)/shard_map/all_to_all | solution.py:52
  16.6 0.0 reduce-scatter.3.cloned.1.call-start
  16.6 0.7 slice_bitcast_fusion.1
  17.4 6.1 %copy.24 = bf16[3,3,3,256,256]{3,4,2,1,0:T(8,128)(2,1)} copy(bf16[3,3,3,256,256]{4,3,2,1,0:T(8,128)(2,1)} %param.9) | data formatting | bytes 7077888 | tf_op args[1]
  23.5 4.2 %reverse_bitcast_fusion = bf16[3,3,3,256,256]{4,3,2,1,0:T(8,128)(2,1)} fusion(bf16[3,3,3,256,256]{3,4,2,1,0:T(8,128)(2,1)} %copy.24), kind=kLoop, calls=%fused_computation.180 | loop fusion | bytes 7077888 | tf_op jit(solution)/shard_map/transpose | solution.py:65
  27.7 0.0 copy-done.2
  27.7 4.1 %rev.3 = bf16[3,3,3,256,256]{3,4,2,1,0:T(8,128)(2,1)} reverse(bf16[3,3,3,256,256]{3,4,2,1,0:T(8,128)(2,1)} %copy.24), dimensions={0,1,2} | reverse | bytes 7077888 | tf_op jit(solution)/shard_map/rev | solution.py:65
  31.8 0.0 collective-permute-done
  31.8 0.1 pad_maximum_fusion
  31.9 1.3 pad_slice_fusion.48
  33.2 0.8 pad_slice_fusion.49
  34.0 0.1 fusion.5
  34.1 0.6 concatenate.77
  34.8 0.0 copy-start.3
  34.8 1.5 %concatenate.78 = bf16[128,256]{1,0:T(8,128)(2,1)} reshape(bf16[4,8,4,256]{3,2,1,0:T(4,128)(2,1)} %get-tuple-element.33) | data formatting | bytes 131072 | tf_op jit(solution)/shard_map/concatenate | solution.py:28
  36.3 1.5 %concatenate.79 = bf16[128,256]{1,0:T(8,128)(2,1)} reshape(bf16[4,8,4,256]{3,2,1,0:T(4,128)(2,1)} %get-tuple-element.34) | data formatting | bytes 131072 | tf_op jit(solution)/shard_map/concatenate | solution.py:28
  37.8 0.6 concatenate.80
  38.4 1.5 %concatenate.81 = bf16[128,256]{1,0:T(8,128)(2,1)} reshape(bf16[4,8,4,256]{3,2,1,0:T(4,128)(2,1)} %get-tuple-element.35) | data formatting | bytes 131072 | tf_op jit(solution)/shard_map/concatenate | solution.py:28
  39.9 1.5 %concatenate.82 = bf16[128,256]{1,0:T(8,128)(2,1)} reshape(bf16[4,8,4,256]{3,2,1,0:T(4,128)(2,1)} %get-tuple-element.36) | data formatting | bytes 131072 | tf_op jit(solution)/shard_map/concatenate | solution.py:28
  41.4 1.5 %concatenate.83 = bf16[128,256]{1,0:T(8,128)(2,1)} reshape(bf16[4,8,4,256]{3,2,1,0:T(4,128)(2,1)} %get-tuple-element.37) | data formatting | bytes 131072 | tf_op jit(solution)/shard_map/concatenate | solution.py:28
  42.9 1.5 %concatenate.84 = bf16[128,256]{1,0:T(8,128)(2,1)} reshape(bf16[4,8,4,256]{3,2,1,0:T(4,128)(2,1)} %get-tuple-element.38) | data formatting | bytes 131072 | tf_op jit(solution)/shard_map/concatenate | solution.py:28
  44.4 1.5 %concatenate.85 = bf16[128,256]{1,0:T(8,128)(2,1)} reshape(bf16[4,8,4,256]{3,2,1,0:T(4,128)(2,1)} %get-tuple-element.39) | data formatting | bytes 131072 | tf_op jit(solution)/shard_map/concatenate | solution.py:28
  45.9 0.6 concatenate.86
  46.5 0.6 concatenate.87
  47.4 0.9 concatenate.99
  48.3 0.0 copy-done.4
  48.3 0.0 copy-done.3
  48.4 0.9 concatenate.102
  49.2 0.8 constant_dynamic-update-slice_fusion.52
  50.1 0.8 constant_dynamic-update-slice_fusion.51
  50.9 0.8 constant_dynamic-update-slice_fusion.50
  51.8 0.8 constant_dynamic-update-slice_fusion.49
  52.6 0.8 constant_dynamic-update-slice_fusion.48
  53.4 0.8 constant_dynamic-update-slice_fusion.47
  54.3 0.8 constant_dynamic-update-slice_fusion.46
  55.1 0.8 constant_dynamic-update-slice_fusion.45
  56.0 0.8 constant_dynamic-update-slice_fusion.44
  56.8 0.8 constant_dynamic-update-slice_fusion.43
  57.7 0.8 constant_dynamic-update-slice_fusion.42
  58.7 2.6 %fusion.10 = f32[128,256]{1,0:T(8,128)S(1)} fusion(bf16[128,6912]{1,0:T(8,128)(2,1)S(1)} %constant_dynamic-update-slice_fusion.27, bf16[6912,256]{1,0:T(8,128)(2,1)} %bitcast.37), kind=kOutput, calls=%fused_computation.182 | convolution fusion | flops 452984832 | bytes 5439488 | tf_op jit(solution)/shard_map/dot_general | solution.py:31
  61.4 0.0 all-to-all-done
  61.4 0.1 copy.33
  61.5 0.1 reshape.116
  61.5 0.0 copy-done
  61.6 0.3 fusion.2
  61.9 1.3 fusion.3
  63.3 1.3 collective-permute-start.1
  64.6 0.0 reduce-scatter.3.cloned.1.call-update
  64.6 0.0 reduce-scatter.5.cloned.1.call-start
  64.6 4.0 %conditional.1 = (f32[1,8,4,256]{3,1,2,0:T(8,128)S(1)}) conditional(s32[]{:T(128)} %convert_element_type.26, () %tuple.20, (bf16[4,8,4,256]{3,2,1,0:T(4,128)(2,1)S(1)}, bf16[3,3,3,256,256]{4,3,2,1,0:T(8,128)(2,1)}) %tuple.21), branch_computations={%region_0.1_spmd, %region_1.2_spmd} | conditional | flops 226500608 | bytes 9175050 | solution.py:79
  65.7 0.2 reshape.110
  65.9 2.7 %fusion.9 = f32[64,256]{1,0:T(8,128)S(1)} fusion(bf16[64,6912]{1,0:T(8,128)(2,1)S(1)} %reshape.110, bf16[6912,256]{1,0:T(8,128)(2,1)} %bitcast.36), kind=kOutput, calls=%fused_computation.181 | convolution fusion | flops 226492416 | bytes 4489216 | tf_op jit(solution)/shard_map/cond/branch_1_fun/dot_general | solution.py:31
  68.7 0.0 collective-permute-done.1
  68.8 0.0 copy-start.1
  69.3 1.5 %copy-done.1 = bf16[3,3,3,256,256]{3,4,2,1,0:T(8,128)(2,1)S(1)} copy-done((bf16[3,3,3,256,256]{3,4,2,1,0:T(8,128)(2,1)S(1)}, bf16[3,3,3,256,256]{3,4,2,1,0:T(8,128)(2,1)}, u32[]{:S(2)}) %copy-start.1) | copy-done | bytes 3538968
  70.8 0.7 fusion.11
  71.5 28.2 %reduce-scatter.3.cloned.1.call-done = f32[32,1024]{1,0:T(8,128)} async-done(((f32[256,1024]{1,0:T(8,128)}), f32[32,1024]{1,0:T(8,128)}) %reduce-scatter.3.cloned.1.call-update) | async-done | bytes 131088 | tf_op jit(solution)/shard_map/reduce_scatter | solution.py:84
  99.7 0.0 reduce-scatter.5.cloned.1.call-update
  99.8 0.7 copy.26
  100.4 24.3 %reduce-scatter.5.cloned.1.call-done = f32[32,256]{1,0:T(8,128)} async-done(((f32[32,1024]{1,0:T(8,128)}), f32[32,256]{1,0:T(8,128)}) %reduce-scatter.5.cloned.1.call-update) | async-done | bytes 32784 | tf_op jit(solution)/shard_map/reduce_scatter | solution.py:85
  124.8 1.4 %broadcast_multiply_fusion = f32[32,256]{1,0:T(8,128)} fusion(f32[32,256]{1,0:T(8,128)} %reduce-scatter.5.cloned.1.call-done), kind=kLoop, calls=%fused_computation.177 | loop fusion | flops 8192 | bytes 65536 | tf_op jit(solution)/shard_map/mul | solution.py:86
  (100 shorter events, 1.8 us)
Async XLA Ops:
  7.2 54.4 %copy-start = (bf16[256,1024]{1,0:T(8,128)(2,1)S(1)}, bf16[256,1024]{1,0:T(8,128)(2,1)}, u32[]{:S(2)}) copy-start(bf16[256,1024]{1,0:T(8,128)(2,1)} %param.10) | copy-start | bytes 1572868
  8.0 23.8 %collective-permute-start = (bf16[2,8,4,256]{3,2,1,0:T(4,128)(2,1)S(1)}, bf16[2,8,4,256]{3,2,1,0:T(4,128)(2,1)S(1)}, u32[]{:S(2)}, u32[]{:S(2)}) collective-permute-start(bf16[2,8,4,256]{3,2,1,0:T(4,128)(2,1)S(1)} %slice_bitcast_fusion), channel_id=1, source_target_pairs={{0,4},{4,8},{8,12},{12,16},{16,20},{20,24},{24,28},{1,5},{5,9},{9,... | collective-permute-start | bytes 98312 | tf_op jit(solution)/shard_map/ppermute | solution.py:11
  10.4 50.9 %all-to-all-start = ((bf16[1,32,1,4,1024]{4,3,2,0,1:T(4,128)(2,1)}), bf16[1,32,1,4,1024]{4,3,2,0,1:T(4,128)(2,1)S(1)}, u32[]{:S(2)}, u32[]{:S(2)}) async-start(bf16[1,32,1,4,1024]{4,3,2,0,1:T(4,128)(2,1)} %bitcast.45), calls=%async_computation | async-start | bytes 524288 | tf_op jit(solution)/shard_map/all_to_all | solution.py:52
  16.6 83.1 %reduce-scatter.3.cloned.1.call-start = ((), (), s32[]{:S(2)}) async-start(), calls=%async_computation.3 | async-start | bytes 1179648 | tf_op jit(solution)/shard_map/reduce_scatter | solution.py:84
  23.5 4.2 %copy-start.2 = (bf16[1,4,8,4,256]{4,3,2,1,0:T(4,128)(2,1)S(1)}, bf16[1,4,8,4,256]{4,3,2,1,0:T(4,128)(2,1)}, u32[]{:S(2)}) copy-start(bf16[1,4,8,4,256]{4,3,2,1,0:T(4,128)(2,1)} %param.8) | copy-start | bytes 196612
  34.8 13.6 %copy-start.3 = (bf16[4,8,4,256]{3,2,1,0:T(4,128)(2,1)S(1)}, bf16[4,8,4,256]{3,2,1,0:T(4,128)(2,1)}, u32[]{:S(2)}) copy-start(bf16[4,8,4,256]{3,2,1,0:T(4,128)(2,1)} %get-tuple-element.50) | copy-start | bytes 196612
  38.4 9.9 %copy-start.4 = (bf16[4,8,4,256]{3,2,1,0:T(4,128)(2,1)S(1)}, bf16[4,8,4,256]{3,2,1,0:T(4,128)(2,1)}, u32[]{:S(2)}) copy-start(bf16[4,8,4,256]{3,2,1,0:T(4,128)(2,1)} %get-tuple-element.53) | copy-start | bytes 196612
  63.3 5.4 %collective-permute-start.1 = (bf16[2,8,4,256]{3,1,2,0:T(8,128)(2,1)S(1)}, bf16[2,8,4,256]{3,1,2,0:T(8,128)(2,1)S(1)}, u32[]{:S(2)}, u32[]{:S(2)}) collective-permute-start(bf16[2,8,4,256]{3,1,2,0:T(8,128)(2,1)S(1)} %copy.21), channel_id=1, source_target_pairs={{4,0},{8,4},{12,8},{16,12},{20,16},{24,20},{28,24},{5,1},{9,5},{13... | collective-permute-start | bytes 98312 | tf_op jit(solution)/shard_map/ppermute | solution.py:11
  64.6 60.2 %reduce-scatter.5.cloned.1.call-start = ((), (), s32[]{:S(2)}) async-start(), calls=%async_computation.4 | async-start | bytes 163840 | tf_op jit(solution)/shard_map/reduce_scatter | solution.py:85
  68.8 2.0 %copy-start.1 = (bf16[3,3,3,256,256]{3,4,2,1,0:T(8,128)(2,1)S(1)}, bf16[3,3,3,256,256]{3,4,2,1,0:T(8,128)(2,1)}, u32[]{:S(2)}) copy-start(bf16[3,3,3,256,256]{3,4,2,1,0:T(8,128)(2,1)} %rev.3) | copy-start | bytes 10616836
Sparse Core Ops, SparseCore 0:
  64.7 34.9 reduce-scatter.2
  102.4 22.2 reduce-scatter.4
where the time goes:
time: 135 us; the launch traced here: 133 us
  waiting for transfers between devices  52.6 us (39%)
  local copies, waits for them, and re-layouts  46.5 us (34%)
  between operations  14.6 us (11%)
  starting transfers between devices  9.93 us (7%)
  matrix products  7.64 us (6%)
  other arithmetic  1.54 us (1%)
    reduce_scatter x1, waiting for transfers between devices, local(): part = lax.psum_scatter(term, 'tm', scatter_dimension=0, tiled=True)  28.2 us
    reduce_scatter x1, waiting for transfers between devices, local(): lax.psum_scatter(part, ('dp', 'rep'), scatter_dimension=1, tiled=True)  24.3 us
    unnamed x65, local copies, waits for them, and re-layouts  18.1 us
    concatenate x30, local copies, waits for them, and re-layouts, correlate(): stacked = jnp.concatenate(patches, axis=-1)  15.1 us
    all_to_all x1, starting transfers between devices, local(): lax.all_to_all(cotangent, 'tm', split_axis=1, concat_axis=2, tiled=True)  6.16 us
    dot_general x3, matrix products, correlate(): jnp.dot(stacked.reshape(-1, width), flat_kernel, preferred_element_type=j...  6.01 us
    transpose x1, local copies, waits for them, and re-layouts, local(): back_kernel = jnp.transpose(conv_weight[::-1, ::-1, ::-1], (0, 1, 2, 4, 3))  4.21 us
    rev x1, local copies, waits for them, and re-layouts, local(): back_kernel = jnp.transpose(conv_weight[::-1, ::-1, ::-1], (0, 1, 2, 4, 3))  4.13 us
  transfers between devices with their start and end apart: 5, of which 2 were waited for; matrix products, arithmetic and copies ran while one was open for 38% of the time, Pallas kernels for 0%

commit v1 on v0

--- a/solution.py
+++ b/solution.py
@@ -49,7 +49,13 @@
     hidden = jax.nn.silu(pre).astype(jnp.bfloat16).reshape(1, frames, rows, cols, chans)
     contract_rows = (((0,), (0,)), ((), ()))
     contract_cols = (((1,), (1,)), ((), ()))
-    frame_cot = lax.all_to_all(cotangent, "tm", split_axis=1, concat_axis=2, tiled=True)
+
+    def direct_skins_for(shard_in):
+        return jnp.concatenate(
+            lax.all_to_all(jnp.stack(jnp.split(shard_in, lax.axis_size("tm"), 1)), "tm", 0, 0), 2
+        )
+
+    frame_cot = direct_skins_for(cotangent)
     flat_g = frame_cot.reshape(-1, frame_cot.shape[-1])
     term = lax.dot_general(
         hidden.reshape(-1, chans), flat_g, contract_rows, preferred_element_type=jnp.float32

time: 135 us -> 147 us (1.089)
  local copies, waits for them, and re-layouts: 46.5 us -> 58.3 us
    unnamed x65 -> x70, local copies, waits for them, and re-layouts: 18.1 us -> 27.6 us
    concatenate x30, local copies, waits for them, and re-layouts: 15.1 us -> 16.7 us  [correlate(): stacked = jnp.concatenate(patches, axis=-1)]
  transfers between devices with their start and end apart: 5 -> 5, of which waited for: 2 -> 2; matrix products, arithmetic and copies ran while one was open for 38% -> 43% of each run, Pallas kernels for 0% -> 0%
where the time goes in v1:
time: 147 us; the launch traced here: 145 us
  local copies, waits for them, and re-layouts  58.3 us (40%)
  waiting for transfers between devices  52.7 us (36%)
  between operations  14.6 us (10%)
  starting transfers between devices  9.91 us (7%)
  matrix products  7.63 us (5%)
  other arithmetic  1.54 us (1%)
    reduce_scatter x1, waiting for transfers between devices, local(): part = lax.psum_scatter(term, 'tm', scatter_dimension=0, tiled=True)  28.2 us
    unnamed x70, local copies, waits for them, and re-layouts  27.6 us
    reduce_scatter x1, waiting for transfers between devices, local(): lax.psum_scatter(part, ('dp', 'rep'), scatter_dimension=1, tiled=True)  24.4 us
    concatenate x30, local copies, waits for them, and re-layouts, correlate(): stacked = jnp.concatenate(patches, axis=-1)  16.7 us
    all_to_all x1, starting transfers between devices, direct_skins_for(): lax.all_to_all(jnp.stack(jnp.split(shard_in, lax.axis_size('tm'), 1)), 't...  6.15 us
    dot_general x3, matrix products, correlate(): jnp.dot(stacked.reshape(-1, width), flat_kernel, preferred_element_type=j...  6.01 us
    transpose x1, local copies, waits for them, and re-layouts, local(): back_kernel = jnp.transpose(conv_weight[::-1, ::-1, ::-1], (0, 1, 2, 4, 3))  4.2 us
    rev x1, local copies, waits for them, and re-layouts, local(): back_kernel = jnp.transpose(conv_weight[::-1, ::-1, ::-1], (0, 1, 2, 4, 3))  4.13 us
  transfers between devices with their start and end apart: 5, of which 2 were waited for; matrix products, arithmetic and copies ran while one was open for 43% of the time, Pallas kernels for 0%

profile of v1, /device:TPU:0, one launch (start us, length us, event | category | flops | bytes accessed | tf_op | source)
XLA Modules:
  0.0 144.8 jit_solution(3468411157536217187)
XLA Ops:
  7.2 0.0 copy-start
  7.2 0.8 slice_bitcast_fusion.7
  8.0 2.4 %collective-permute-start = (bf16[2,8,4,256]{3,2,1,0:T(4,128)(2,1)S(1)}, bf16[2,8,4,256]{3,2,1,0:T(4,128)(2,1)S(1)}, u32[]{:S(2)}, u32[]{:S(2)}) collective-permute-start(bf16[2,8,4,256]{3,2,1,0:T(4,128)(2,1)S(1)} %slice_bitcast_fusion.7), channel_id=1, source_target_pairs={{0,4},{4,8},{8,12},{12,16},{16,20},{20,24},{24,28},{1,5},{5,9},{9,... | collective-permute-start | bytes 98312 | tf_op jit(solution)/shard_map/ppermute | solution.py:11
  10.4 1.4 constant_dynamic-update-slice_fusion.34
  11.8 1.4 constant_dynamic-update-slice_fusion.33
  13.2 1.4 constant_dynamic-update-slice_fusion.32
  14.5 1.4 constant_dynamic-update-slice_fusion.31
  15.9 1.4 constant_dynamic-update-slice_fusion.30
  17.3 1.4 constant_dynamic-update-slice_fusion.29
  18.6 1.4 constant_dynamic-update-slice_fusion.28
  20.0 1.4 constant_dynamic-update-slice_fusion.27
  21.4 6.1 %all-to-all-start = ((bf16[8,1,4,1,4,1024]{5,4,2,3,1,0:T(4,128)(2,1)}), bf16[8,1,4,1,4,1024]{5,4,2,3,1,0:T(4,128)(2,1)S(1)}, u32[]{:S(2)}, u32[]{:S(2)}) async-start(bf16[8,1,4,1,4,1024]{5,4,2,3,1,0:T(4,128)(2,1)} %constant_dynamic-update-slice_fusion.27), calls=%async_computation | async-start | bytes 524288 | tf_op jit(solution)/shard_map/all_to_all | solution.py:55
  27.5 0.0 reduce-scatter.3.cloned.1.call-start
  27.6 0.7 slice_bitcast_fusion.8
  28.3 6.1 %copy.30 = bf16[3,3,3,256,256]{3,4,2,1,0:T(8,128)(2,1)} copy(bf16[3,3,3,256,256]{4,3,2,1,0:T(8,128)(2,1)} %param.9) | data formatting | bytes 7077888 | tf_op args[1]
  34.4 4.2 %reverse_bitcast_fusion = bf16[3,3,3,256,256]{4,3,2,1,0:T(8,128)(2,1)} fusion(bf16[3,3,3,256,256]{3,4,2,1,0:T(8,128)(2,1)} %copy.30), kind=kLoop, calls=%fused_computation.194 | loop fusion | bytes 7077888 | tf_op jit(solution)/shard_map/transpose | solution.py:71
  38.6 4.1 %rev.3 = bf16[3,3,3,256,256]{3,4,2,1,0:T(8,128)(2,1)} reverse(bf16[3,3,3,256,256]{3,4,2,1,0:T(8,128)(2,1)} %copy.30), dimensions={0,1,2} | reverse | bytes 7077888 | tf_op jit(solution)/shard_map/rev | solution.py:71
  42.7 0.0 collective-permute-done
  42.8 0.1 pad_maximum_fusion
  42.8 1.3 pad_slice_fusion.48
  44.1 0.2 pad_slice_fusion.49
  44.3 0.1 fusion.5
  44.4 0.6 concatenate.77
  45.1 1.5 %concatenate.78 = bf16[128,256]{1,0:T(8,128)(2,1)} reshape(bf16[4,8,4,256]{3,2,1,0:T(4,128)(2,1)} %get-tuple-element.31) | data formatting | bytes 131072 | tf_op jit(solution)/shard_map/concatenate | solution.py:28
  46.6 1.5 %concatenate.79 = bf16[128,256]{1,0:T(8,128)(2,1)} reshape(bf16[4,8,4,256]{3,2,1,0:T(4,128)(2,1)} %get-tuple-element.32) | data formatting | bytes 131072 | tf_op jit(solution)/shard_map/concatenate | solution.py:28
  48.0 0.6 concatenate.80
  48.7 1.5 %concatenate.81 = bf16[128,256]{1,0:T(8,128)(2,1)} reshape(bf16[4,8,4,256]{3,2,1,0:T(4,128)(2,1)} %get-tuple-element.33) | data formatting | bytes 131072 | tf_op jit(solution)/shard_map/concatenate | solution.py:28
  50.2 1.5 %concatenate.82 = bf16[128,256]{1,0:T(8,128)(2,1)} reshape(bf16[4,8,4,256]{3,2,1,0:T(4,128)(2,1)} %get-tuple-element.34) | data formatting | bytes 131072 | tf_op jit(solution)/shard_map/concatenate | solution.py:28
  51.6 1.5 %concatenate.83 = bf16[128,256]{1,0:T(8,128)(2,1)} reshape(bf16[4,8,4,256]{3,2,1,0:T(4,128)(2,1)} %get-tuple-element.35) | data formatting | bytes 131072 | tf_op jit(solution)/shard_map/concatenate | solution.py:28
  53.1 1.5 %concatenate.84 = bf16[128,256]{1,0:T(8,128)(2,1)} reshape(bf16[4,8,4,256]{3,2,1,0:T(4,128)(2,1)} %get-tuple-element.36) | data formatting | bytes 131072 | tf_op jit(solution)/shard_map/concatenate | solution.py:28
  54.6 1.5 %concatenate.85 = bf16[128,256]{1,0:T(8,128)(2,1)} reshape(bf16[4,8,4,256]{3,2,1,0:T(4,128)(2,1)} %get-tuple-element.37) | data formatting | bytes 131072 | tf_op jit(solution)/shard_map/concatenate | solution.py:28
  56.1 1.5 %concatenate.86 = bf16[128,256]{1,0:T(8,128)(2,1)} reshape(bf16[4,8,4,256]{3,2,1,0:T(4,128)(2,1)} %get-tuple-element.38) | data formatting | bytes 131072 | tf_op jit(solution)/shard_map/concatenate | solution.py:28
  57.5 1.5 %concatenate.87 = bf16[128,256]{1,0:T(8,128)(2,1)} reshape(bf16[4,8,4,256]{3,2,1,0:T(4,128)(2,1)} %get-tuple-element.39) | data formatting | bytes 131072 | tf_op jit(solution)/shard_map/concatenate | solution.py:28
  59.0 0.9 concatenate.88
  60.2 0.9 concatenate.102
  61.0 0.8 constant_dynamic-update-slice_fusion.60
  61.9 0.8 constant_dynamic-update-slice_fusion.59
  62.7 0.8 constant_dynamic-update-slice_fusion.58
  63.6 0.8 constant_dynamic-update-slice_fusion.57
  64.4 0.8 constant_dynamic-update-slice_fusion.56
  65.3 0.8 constant_dynamic-update-slice_fusion.55
  66.1 0.8 constant_dynamic-update-slice_fusion.54
  67.0 0.8 constant_dynamic-update-slice_fusion.53
  67.8 0.8 constant_dynamic-update-slice_fusion.52
  68.6 0.8 constant_dynamic-update-slice_fusion.51
  69.5 0.8 constant_dynamic-update-slice_fusion.50
  70.5 2.6 %fusion.10 = f32[128,256]{1,0:T(8,128)S(1)} fusion(bf16[128,6912]{1,0:T(8,128)(2,1)S(1)} %constant_dynamic-update-slice_fusion.35, bf16[6912,256]{1,0:T(8,128)(2,1)} %bitcast.70), kind=kOutput, calls=%fused_computation.196 | convolution fusion | flops 452984832 | bytes 5439488 | tf_op jit(solution)/shard_map/dot_general | solution.py:31
  73.2 0.1 copy.26
  73.3 0.1 reshape_reshape.3
  73.4 0.3 fusion.2
  73.7 1.3 fusion.3
  75.1 1.3 collective-permute-start.1
  76.4 0.0 reduce-scatter.3.cloned.1.call-update
  76.4 0.0 reduce-scatter.5.cloned.1.call-start
  76.5 4.0 %conditional.1 = (f32[1,8,4,256]{3,1,2,0:T(8,128)S(1)}) conditional(s32[]{:T(128)} %convert_element_type.26, () %tuple.20, (bf16[4,8,4,256]{3,2,1,0:T(4,128)(2,1)S(1)}, bf16[3,3,3,256,256]{4,3,2,1,0:T(8,128)(2,1)}) %tuple.21), branch_computations={%region_0.1_spmd, %region_1.2_spmd} | conditional | flops 226500608 | bytes 9175050 | solution.py:85
  77.5 0.2 reshape.109
  77.7 2.7 %fusion.9 = f32[64,256]{1,0:T(8,128)S(1)} fusion(bf16[64,6912]{1,0:T(8,128)(2,1)S(1)} %reshape.109, bf16[6912,256]{1,0:T(8,128)(2,1)} %bitcast.69), kind=kOutput, calls=%fused_computation.195 | convolution fusion | flops 226492416 | bytes 4489216 | tf_op jit(solution)/shard_map/cond/branch_1_fun/dot_general | solution.py:31
  81.1 1.5 %copy-done.1 = bf16[3,3,3,256,256]{3,4,2,1,0:T(8,128)(2,1)S(1)} copy-done((bf16[3,3,3,256,256]{3,4,2,1,0:T(8,128)(2,1)S(1)}, bf16[3,3,3,256,256]{3,4,2,1,0:T(8,128)(2,1)}, u32[]{:S(2)}) %copy-start.1) | copy-done | bytes 3538968
  82.6 0.7 fusion.11
  83.3 28.2 %reduce-scatter.3.cloned.1.call-done = f32[32,1024]{1,0:T(8,128)} async-done(((f32[256,1024]{1,0:T(8,128)}), f32[32,1024]{1,0:T(8,128)}) %reduce-scatter.3.cloned.1.call-update) | async-done | bytes 131088 | tf_op jit(solution)/shard_map/reduce_scatter | solution.py:90
  111.5 0.0 reduce-scatter.5.cloned.1.call-update
  111.5 0.7 copy.32
  112.2 24.4 %reduce-scatter.5.cloned.1.call-done = f32[32,256]{1,0:T(8,128)} async-done(((f32[32,1024]{1,0:T(8,128)}), f32[32,256]{1,0:T(8,128)}) %reduce-scatter.5.cloned.1.call-update) | async-done | bytes 32784 | tf_op jit(solution)/shard_map/reduce_scatter | solution.py:91
  136.6 1.4 broadcast_multiply_fusion
  (106 shorter events, 1.8 us)
Async XLA Ops:
  7.2 66.2 %copy-start = (bf16[256,1024]{1,0:T(8,128)(2,1)S(1)}, bf16[256,1024]{1,0:T(8,128)(2,1)}, u32[]{:S(2)}) copy-start(bf16[256,1024]{1,0:T(8,128)(2,1)} %param.10) | copy-start | bytes 1572868
  8.0 34.7 %collective-permute-start = (bf16[2,8,4,256]{3,2,1,0:T(4,128)(2,1)S(1)}, bf16[2,8,4,256]{3,2,1,0:T(4,128)(2,1)S(1)}, u32[]{:S(2)}, u32[]{:S(2)}) collective-permute-start(bf16[2,8,4,256]{3,2,1,0:T(4,128)(2,1)S(1)} %slice_bitcast_fusion.7), channel_id=1, source_target_pairs={{0,4},{4,8},{8,12},{12,16},{16,20},{20,24},{24,28},{1,5},{5,9},{9,... | collective-permute-start | bytes 98312 | tf_op jit(solution)/shard_map/ppermute | solution.py:11
  21.4 51.8 %all-to-all-start = ((bf16[8,1,4,1,4,1024]{5,4,2,3,1,0:T(4,128)(2,1)}), bf16[8,1,4,1,4,1024]{5,4,2,3,1,0:T(4,128)(2,1)S(1)}, u32[]{:S(2)}, u32[]{:S(2)}) async-start(bf16[8,1,4,1,4,1024]{5,4,2,3,1,0:T(4,128)(2,1)} %constant_dynamic-update-slice_fusion.27), calls=%async_computation | async-start | bytes 524288 | tf_op jit(solution)/shard_map/all_to_all | solution.py:55
  27.5 83.9 %reduce-scatter.3.cloned.1.call-start = ((), (), s32[]{:S(2)}) async-start(), calls=%async_computation.3 | async-start | bytes 1179648 | tf_op jit(solution)/shard_map/reduce_scatter | solution.py:90
  34.4 4.2 %copy-start.2 = (bf16[1,4,8,4,256]{4,3,2,1,0:T(4,128)(2,1)S(1)}, bf16[1,4,8,4,256]{4,3,2,1,0:T(4,128)(2,1)}, u32[]{:S(2)}) copy-start(bf16[1,4,8,4,256]{4,3,2,1,0:T(4,128)(2,1)} %param.8) | copy-start | bytes 196612
  45.0 15.0 %copy-start.3 = (bf16[4,8,4,256]{3,2,1,0:T(4,128)(2,1)S(1)}, bf16[4,8,4,256]{3,2,1,0:T(4,128)(2,1)}, u32[]{:S(2)}) copy-start(bf16[4,8,4,256]{3,2,1,0:T(4,128)(2,1)} %get-tuple-element.47) | copy-start | bytes 196612
  75.1 5.4 %collective-permute-start.1 = (bf16[2,8,4,256]{3,1,2,0:T(8,128)(2,1)S(1)}, bf16[2,8,4,256]{3,1,2,0:T(8,128)(2,1)S(1)}, u32[]{:S(2)}, u32[]{:S(2)}) collective-permute-start(bf16[2,8,4,256]{3,1,2,0:T(8,128)(2,1)S(1)} %copy.27), channel_id=1, source_target_pairs={{4,0},{8,4},{12,8},{16,12},{20,16},{24,20},{28,24},{5,1},{9,5},{13... | collective-permute-start | bytes 98312 | tf_op jit(solution)/shard_map/ppermute | solution.py:11
  76.4 60.2 %reduce-scatter.5.cloned.1.call-start = ((), (), s32[]{:S(2)}) async-start(), calls=%async_computation.4 | async-start | bytes 163840 | tf_op jit(solution)/shard_map/reduce_scatter | solution.py:91
  80.6 2.0 %copy-start.1 = (bf16[3,3,3,256,256]{3,4,2,1,0:T(8,128)(2,1)S(1)}, bf16[3,3,3,256,256]{3,4,2,1,0:T(8,128)(2,1)}, u32[]{:S(2)}) copy-start(bf16[3,3,3,256,256]{3,4,2,1,0:T(8,128)(2,1)} %rev.3) | copy-start | bytes 10616836
Sparse Core Ops, SparseCore 0:
  76.5 34.8 reduce-scatter.2
  114.2 22.3 reduce-scatter.4
